TPU v7x, 32 devices: a whole 2x2x4 slice. The times are simulated.
32 devices in a mesh: ctx: 8 (over z, x), head: 4 (over y, core).
Axes of the slice: x: 2, y: 2, z: 4, core: 2. Of those that a mesh axis runs over, the one named last changes fastest.
Arguments:
- token_keys: bfloat16 [8, 2048, 128], P(None, ('ctx', 'head')), may hold values from -4.5 to 4.5
- token_values: bfloat16 [8, 2048, 128], P(None, ('ctx', 'head')), may hold values from -6 to 6
- queries: bfloat16 [8, 2048, 8, 128], P(None, ('ctx', 'head')), may hold values from -16 to 16
- out_grad: bfloat16 [8, 2048, 8, 128], P(None, ('ctx', 'head')), may hold values from -6 to 6
- slot_ids: int32 [8, 2048], P('head'), may hold values from 0 to 511, as said below
Outputs:
- attended: bfloat16 [8, 2048, 8, 128], P(None, ('ctx', 'head'))
- key_grad: float32 [8, 2048, 128], P(None, ('ctx', 'head'))
- value_grad: float32 [8, 2048, 128], P(None, ('ctx', 'head'))
Inputs may be any that keep to these rules, and one draw needn't show every extreme that they name: `slot_ids`: in each head's row slot numbers never fall; each of the 512 slots holds 1 to 16 consecutive tokens; slots k * 64 to (k + 1) * 64 - 1 all begin among tokens k * 256 to (k + 1) * 256 - 1; every such block of tokens holds a slot of exactly 16 tokens.
All inputs are finite; a program needn't handle non-finite values.
Results may differ from a plain program's by a relative error of at most 0.012.
The roundings to bfloat16 on the way count: a program that leaves them out, or rounds other values in their place, can miss the bound.
Values may be sent and summed in bfloat16 or wider, within the bound.
A program may use at most 64 MiB of HBM per device.

v0:
```python
import math
import jax
import jax.numpy as jnp
from jax import lax
from jax.sharding import PartitionSpec as P

RATIO = 4
neg_big = -1e30


def from_behind(value, axis, steps):
    count = lax.axis_size(axis)
    initial, last = (max(0, -steps), min(count, count - steps))
    return lax.ppermute(value, axis, [(source, source + steps) for source in range(initial, last)])


def one_hot_rows(own_ids, first_row, how_many):
    relative = own_ids - first_row
    columns = jnp.arange(how_many, dtype=jnp.int32)
    return (relative[:, :, None] == columns[None, None, :]).astype(jnp.bfloat16)


def per_device(token_keys, token_values, queries, out_grad, slot_ids):
    keys_here, values_here, query_here, grad_here = (
        lax.all_to_all(token_keys, "head", split_axis=0, concat_axis=1, tiled=True),
        lax.all_to_all(token_values, "head", split_axis=0, concat_axis=1, tiled=True),
        lax.all_to_all(queries, "head", split_axis=0, concat_axis=1, tiled=True),
        lax.all_to_all(out_grad, "head", split_axis=0, concat_axis=1, tiled=True),
    )
    local_heads, tok_count, head_dim = keys_here.shape
    query_count = query_here.shape[1]
    group_size = query_here.shape[2]
    slot_count = tok_count // RATIO
    id_heads, context_len = slot_ids.shape
    total_slots = context_len // RATIO
    block_count = context_len // tok_count
    ctx_index = lax.axis_index("ctx")
    blocked_ids = slot_ids.reshape(id_heads, block_count, tok_count)
    block_base = jnp.arange(block_count, dtype=jnp.int32)
    targets = block_base[:, None] * slot_count + jnp.arange(slot_count, dtype=jnp.int32)[None, :]
    below_count = jnp.sum(
        (blocked_ids[:, :, :, None] < targets[None, :, None, :]).astype(jnp.int32), axis=2
    )
    starts_all = (block_base[None, :, None] * tok_count + below_count).reshape(
        id_heads, total_slots
    )
    slot_edges = jnp.concatenate(
        [starts_all, jnp.full((id_heads, 1), context_len, jnp.int32)], axis=1
    )
    slot_start = starts_all.T
    slot_len = slot_edges[:, 1:] - slot_edges[:, :-1]
    lengths_t = slot_len.T.astype(jnp.float32)[:, :, None]
    own_ids = lax.dynamic_slice_in_dim(slot_ids, ctx_index * tok_count, tok_count, 1)
    pair_low = jnp.concatenate([keys_here, values_here], axis=2)
    first_slot = ctx_index * slot_count - 1
    hot = one_hot_rows(own_ids, first_slot, slot_count + 1)
    window = jnp.einsum("htn,htc->nhc", hot, pair_low, preferred_element_type=jnp.float32)
    carried = from_behind(window[:1], "ctx", -1)
    padding = jnp.zeros((slot_count - 1, local_heads, 2 * head_dim), jnp.float32)
    own_sums = window[1:] + jnp.concatenate([padding, carried], axis=0)
    own_len = lax.dynamic_slice_in_dim(lengths_t, ctx_index * slot_count, slot_count, 0)
    slot_pairs = (own_sums / own_len).astype(jnp.bfloat16)
    rows_here = query_count * group_size
    query_rows = query_here.reshape(local_heads, rows_here, head_dim)
    grad_rows = grad_here.reshape(local_heads, rows_here, head_dim)
    stride = tok_count // query_count
    positions = jnp.repeat(
        (ctx_index * query_count + jnp.arange(query_count, dtype=jnp.int32)) * stride + stride - 1,
        group_size,
    )
    last_position = (ctx_index + 1) * query_count * stride - 1
    score_scale = 1.0 / math.sqrt(head_dim)

    def block_scores(key_block):
        scores = (
            jnp.einsum("hrd,nhd->hrn", query_rows, key_block, preferred_element_type=jnp.float32)
            * score_scale
        )
        visible = slot_start.T[:, None, :] <= positions[None, :, None]
        return (scores, visible)

    def reaches(first_row):
        return (
            jnp.min(lax.dynamic_index_in_dim(slot_start, first_row, 0, keepdims=False))
            <= last_position
        )

    init_stats = (
        jnp.full((local_heads, rows_here), neg_big, jnp.float32),
        jnp.zeros((local_heads, rows_here), jnp.float32),
    )
    key_block = lax.all_gather(slot_pairs[:, :, :head_dim], "ctx", axis=0, tiled=True)

    def stats_advance(state_in):
        top_now, mass_now = state_in
        scores, visible = block_scores(key_block)
        top_new = jnp.maximum(top_now, jnp.max(jnp.where(visible, scores, neg_big), axis=2))
        fresh = jnp.sum(jnp.where(visible, jnp.exp(scores - top_new[:, :, None]), 0.0), axis=2)
        return (top_new, fresh)

    row_top, row_mass = lax.cond(
        reaches(jnp.int32(0)), stats_advance, lambda state_in: state_in, init_stats
    )
    log_total = row_top + jnp.log(row_mass)

    def weights_of(pair_block):
        scores, visible = block_scores(pair_block[:, :, :head_dim])
        return jnp.where(visible, jnp.exp(scores - log_total[:, :, None]), 0.0)

    init_acc = jnp.zeros((local_heads, rows_here, head_dim), jnp.float32)
    pair_block = lax.all_gather(slot_pairs, "ctx", axis=0, tiled=True)

    def value_advance(state_in):
        weights_low = weights_of(pair_block).astype(jnp.bfloat16)
        return jnp.einsum(
            "hrn,nhd->hrd",
            weights_low,
            pair_block[:, :, head_dim:],
            preferred_element_type=jnp.float32,
        )

    summed_out = lax.cond(reaches(jnp.int32(0)), value_advance, lambda state_in: state_in, init_acc)
    attended = summed_out.astype(jnp.bfloat16)
    out_back = lax.all_to_all(
        attended.reshape(local_heads, query_count, group_size, head_dim),
        "head",
        split_axis=1,
        concat_axis=0,
        tiled=True,
    )
    row_dot = jnp.sum(grad_rows.astype(jnp.float32) * attended.astype(jnp.float32), axis=2)
    init_partials = jnp.zeros((total_slots, local_heads, 2 * head_dim), jnp.float32)
    grad_pair_block = lax.all_gather(slot_pairs, "ctx", axis=0, tiled=True)

    def grad_advance(state_in):
        weights = weights_of(grad_pair_block)
        weights_low = weights.astype(jnp.bfloat16)
        value_grads = jnp.einsum(
            "hrn,hrd->nhd", weights_low, grad_rows, preferred_element_type=jnp.float32
        )
        weight_grads = jnp.einsum(
            "hrd,nhd->hrn",
            grad_rows,
            grad_pair_block[:, :, head_dim:],
            preferred_element_type=jnp.float32,
        )
        dscores = (weights * (weight_grads - row_dot[:, :, None])).astype(jnp.bfloat16)
        key_grads = (
            jnp.einsum("hrn,hrd->nhd", dscores, query_rows, preferred_element_type=jnp.float32)
            * score_scale
        )
        return jnp.concatenate([key_grads, value_grads], axis=2)

    partials = lax.cond(
        reaches(jnp.int32(0)), grad_advance, lambda state_in: state_in, init_partials
    )
    share_grads = lax.psum_scatter(
        partials.astype(jnp.bfloat16), "ctx", scatter_dimension=0, tiled=True
    )
    below_row = from_behind(share_grads[-1:], "ctx", 1)
    grad_window = jnp.concatenate([below_row, share_grads], axis=0)
    hot = one_hot_rows(own_ids, first_slot, grad_window.shape[0])
    token_sums = jnp.einsum("htn,nhc->htc", hot, grad_window, preferred_element_type=jnp.float32)
    padded_len = jnp.concatenate([jnp.ones((id_heads, 1), jnp.int32), slot_len], axis=1)
    window_len = lax.dynamic_slice_in_dim(padded_len, first_slot + 1, slot_count + 1, 1).astype(
        jnp.float32
    )
    relative_ids = own_ids - first_slot
    window_cols = jnp.arange(slot_count + 1, dtype=jnp.int32)
    token_len = jnp.sum(
        jnp.where(
            relative_ids[:, :, None] == window_cols[None, None, :], window_len[:, None, :], 0.0
        ),
        axis=2,
    )[:, :, None]
    token_grads = token_sums / token_len
    key_back, value_back = (
        lax.all_to_all(
            token_grads[:, :, :head_dim].astype(jnp.bfloat16),
            "head",
            split_axis=1,
            concat_axis=0,
            tiled=True,
        ).astype(jnp.float32),
        lax.all_to_all(
            token_grads[:, :, head_dim:].astype(jnp.bfloat16),
            "head",
            split_axis=1,
            concat_axis=0,
            tiled=True,
        ).astype(jnp.float32),
    )
    return (out_back, key_back, value_back)


def solution(mesh):
    placed = (
        P(None, ("ctx", "head"), None),
        P(None, ("ctx", "head"), None),
        P(None, ("ctx", "head"), None, None),
        P(None, ("ctx", "head"), None, None),
        P("head", None),
    )
    return jax.shard_map(
        per_device,
        mesh=mesh,
        in_specs=placed,
        out_specs=(
            P(None, ("ctx", "head"), None, None),
            P(None, ("ctx", "head"), None),
            P(None, ("ctx", "head"), None),
        ),
        check_vma=False,
    )
```

profile of v0, /device:TPU:8, one launch (start us, length us, event | category | flops | bytes accessed | tf_op | source)
XLA Modules:
  0.0 240.5 jit_solution(12412605172236448797)
XLA Ops:
  7.2 3.3 %all-to-all-start = ((bf16[8,64,128]{2,1,0:T(8,128)(2,1)}), bf16[8,64,128]{2,1,0:T(8,128)(2,1)S(1)}, u32[]{:S(2)}, u32[]{:S(2)}) async-start(bf16[8,64,128]{2,1,0:T(8,128)(2,1)} %param.11), calls=%async_computation | async-start | bytes 262144 | tf_op jit(solution)/shard_map/all_to_all | solution.py:25
  12.5 2.6 %all-to-all-done = bf16[8,64,128]{2,1,0:T(8,128)(2,1)S(1)} async-done(((bf16[8,64,128]{2,1,0:T(8,128)(2,1)}), bf16[8,64,128]{2,1,0:T(8,128)(2,1)S(1)}, u32[]{:S(2)}, u32[]{:S(2)}) %all-to-all-start) | async-done | bytes 131104 | tf_op jit(solution)/shard_map/all_to_all | solution.py:25
  15.1 3.3 %all-to-all-start.1 = ((bf16[8,64,128]{2,1,0:T(8,128)(2,1)}), bf16[8,64,128]{2,1,0:T(8,128)(2,1)S(1)}, u32[]{:S(2)}, u32[]{:S(2)}) async-start(bf16[8,64,128]{2,1,0:T(8,128)(2,1)} %param.12), calls=%async_computation.1 | async-start | bytes 262144 | tf_op jit(solution)/shard_map/all_to_all | solution.py:26
  18.5 4.6 %all-to-all-done.1 = bf16[8,64,128]{2,1,0:T(8,128)(2,1)S(1)} async-done(((bf16[8,64,128]{2,1,0:T(8,128)(2,1)}), bf16[8,64,128]{2,1,0:T(8,128)(2,1)S(1)}, u32[]{:S(2)}, u32[]{:S(2)}) %all-to-all-start.1) | async-done | bytes 131104 | tf_op jit(solution)/shard_map/all_to_all | solution.py:26
  23.0 3.5 %all-to-all-start.2 = ((bf16[8,64,8,128]{3,2,1,0:T(8,128)(2,1)}), bf16[8,64,8,128]{3,2,1,0:T(8,128)(2,1)S(1)}, u32[]{:S(2)}, u32[]{:S(2)}) async-start(bf16[8,64,8,128]{3,2,1,0:T(8,128)(2,1)} %param.13), calls=%async_computation.2 | async-start | bytes 2097152 | tf_op jit(solution)/shard_map/all_to_all | solution.py:27
  27.6 13.4 %all-to-all-done.2 = bf16[8,64,8,128]{3,2,1,0:T(8,128)(2,1)S(1)} async-done(((bf16[8,64,8,128]{3,2,1,0:T(8,128)(2,1)}), bf16[8,64,8,128]{3,2,1,0:T(8,128)(2,1)S(1)}, u32[]{:S(2)}, u32[]{:S(2)}) %all-to-all-start.2) | async-done | bytes 1048608 | tf_op jit(solution)/shard_map/all_to_all | solution.py:27
  41.0 4.3 %all-to-all-start.4 = ((bf16[8,64,8,128]{3,2,1,0:T(8,128)(2,1)}), bf16[8,64,8,128]{3,2,1,0:T(8,128)(2,1)}, u32[]{:S(2)}, u32[]{:S(2)}) async-start(bf16[8,64,8,128]{3,2,1,0:T(8,128)(2,1)} %param.14), calls=%async_computation.4 | async-start | bytes 2097152 | tf_op jit(solution)/shard_map/all_to_all | solution.py:28
  45.5 3.3 %collective-permute-start = (f32[1,2,256]{2,0,1:T(1,128)S(1)}, f32[1,2,256]{2,0,1:T(1,128)S(1)}, u32[]{:S(2)}, u32[]{:S(2)}) collective-permute-start(f32[1,2,256]{2,0,1:T(1,128)S(1)} %slice.50), channel_id=1, source_target_pairs={{4,0},{8,4},{12,8},{16,12},{20,16},{24,20},{28,24},{5,1},{9,5},{13... | collective-permute-start | bytes 6152 | tf_op jit(solution)/shard_map/ppermute | solution.py:14
  49.5 1.5 collective-permute-done
  51.1 28.4 %all_gather.8 = bf16[512,2,128]{2,0,1:T(8,128)(2,1)S(1)} all-gather(bf16[64,2,128]{2,0,1:T(8,128)(2,1)S(1)} %slice.51), channel_id=1, replica_groups=mesh['ctx'=8,'head'=4] {'ctx'}, dimensions={0}, use_global_device_ids=true | all-gather | bytes 294912 | tf_op jit(solution)/shard_map/all_gather | solution.py:92
  79.5 31.5 %all_gather.7 = bf16[512,2,256]{2,0,1:T(8,128)(2,1)S(1)} all-gather(bf16[64,2,256]{2,0,1:T(8,128)(2,1)S(1)} %fusion.31), channel_id=1, replica_groups=mesh['ctx'=8,'head'=4] {'ctx'}, dimensions={0}, use_global_device_ids=true | all-gather | bytes 589824 | tf_op jit(solution)/shard_map/all_gather | solution.py:111
  111.1 4.9 %conditional.3 = (f32[2,2048]{1,0:T(2,128)}, f32[2,2048]{1,0:T(2,128)S(1)}) conditional(s32[]{:T(128)} %convert_element_type.72, () %tuple.34, (s32[2,8,64]{2,1,0:T(8,128)S(1)}, s32[256,8]{1,0:T(8,128)S(1)}, bf16[2,2048,128]{2,1,0:T(8,128)(2,1)S(1)}, bf16[512,2,128]{2,0,1:T(8,128)(2,1)S(1)}) %tuple.56), branch_computations={%region_2.3_spmd, %region_3.6_spmd} | conditional | flops 555741184 | bytes 18251792 | solution.py:101
  111.3 1.3 fusion
  113.3 2.7 %fusion.1 = f32[2,2048]{1,0:T(2,128)S(1)} fusion(f32[2,2048,512]{1,2,0:T(8,128)S(1)} %get-tuple-element.122, f32[2,2048]{1,0:T(2,128)} %broadcast_maximum_fusion, s32[2048]{0:T(1024)S(1)} %le.37, s32[2,512]{1,0:T(2,128)S(1)} %le.35), kind=kLoop, calls=%fused_computation.3 | loop fusion | flops 10481664 | bytes 8433664 | tf_op jit(solution)/shard_map/cond/branch_1_fun/reduce_sum | solution.py:98
  116.1 1.3 add.98
  117.4 3.5 %conditional.4 = (bf16[2,2048,128]{2,1,0:T(8,128)(2,1)S(1)}) conditional(s32[]{:T(128)} %convert_element_type.72, () %tuple.33, (s32[2,8,64]{2,1,0:T(8,128)S(1)}, s32[256,8]{1,0:T(8,128)S(1)}, bf16[512,2,256]{2,0,1:T(8,128)(2,1)S(1)}, bf16[2,2048,128]{2,1,0:T(8,128)(2,1)S(1)}, f32[2,2048]{1,0:T(2,128)}) %tuple.57), branch_computations={%region_6.7_spmd, %region_7.8_spmd} | conditional | flops 1084227584 | bytes 2674696 | solution.py:122
  117.6 3.3 %fusion.2 = bf16[2,2048,128]{2,1,0:T(8,128)(2,1)S(1)} fusion(bf16[2,2048,128]{2,1,0:T(8,128)(2,1)S(1)} %get-tuple-element.67, f32[2,2048]{1,0:T(2,128)} %get-tuple-element.69, s32[2,512]{1,0:T(2,128)S(1)} %le.50, s32[2048]{0:T(1024)S(1)} %le.52, bf16[512,2,256]{2,0,1:T(8,128)(2,1)S(1)} %get-tuple-element.68), kind=kOutput, calls=%fused_computation.6 | convolution fusion | flops 1084227584 | bytes 2650112 | tf_op jit(solution)/shard_map/cond/branch_1_fun/hrn,nhd->hrd/dot_general | solution.py:115
  121.1 21.8 %conditional.5 = (bf16[512,2,256]{0,2,1:T(8,128)(2,1)S(1)}) conditional(s32[]{:T(128)} %convert_element_type.72, () %tuple.37, (s32[2,8,64]{2,1,0:T(8,128)S(1)}, s32[256,8]{1,0:T(8,128)S(1)}, bf16[512,2,256]{2,0,1:T(8,128)(2,1)}, bf16[2,2048,128]{2,1,0:T(8,128)(2,1)}, f32[2,2048]{1,0:T(2,128)}, /*index=5*/bf16[2,4,64,8,128]{4,3,2,0,1:T(8,128)(2,1)}, ...), branch_computations={%region_8.9_spmd, %region_9.11_spmd} | conditional | flops 2175528960 | bytes 49414264 | solution.py:154
  122.1 1.3 copy.62
  124.4 5.9 %fusion.20 = f32[2,2048,512]{2,1,0:T(8,128)} fusion(bf16[2,2048,128]{2,1,0:T(8,128)(2,1)} %get-tuple-element.117, bf16[512,2,256]{2,0,1:T(8,128)(2,1)} %get-tuple-element.73), kind=kOutput, calls=%fused_computation.23 | convolution fusion | flops 536870912 | bytes 9699328 | tf_op jit(solution)/shard_map/cond/branch_1_fun/hrd,nhd->hrn/dot_general | solution.py:76
  130.3 7.0 %fusion.17 = bf16[512,2,128]{0,2,1:T(8,128)(2,1)S(1)} fusion(bf16[2,2048,128]{2,1,0:T(8,128)(2,1)S(1)} %copy-done.1, f32[2,2048,512]{2,1,0:T(8,128)} %fusion.20, bf16[2,2048,128]{2,1,0:T(8,128)(2,1)S(1)} %bitcast.57, f32[2,2048]{1,0:T(2,128)S(1)} %multiply_reduce_fusion, f32[2,2048]{1,0:T(2,128)} %get-tuple-element.74, s32[2,512]{1,0:T(2,128)S(1)} %copy-done.5, ...), kind=kOutput, calls=%fused_computation.20 | convolution fusion | flops 1088684032 | bytes 11055104 | tf_op jit(solution)/shard_map/cond/branch_1_fun/hrn,hrd->nhd/dot_general | solution.py:149
  137.2 5.6 %fusion.13 = bf16[512,2,128]{0,2,1:T(8,128)(2,1)S(1)} fusion(bf16[2,2048,128]{2,1,0:T(8,128)(2,1)S(1)} %bitcast.58, f32[2,2048,512]{2,1,0:T(8,128)} %fusion.20, f32[2,2048]{1,0:T(2,128)} %get-tuple-element.74, s32[2,512]{1,0:T(2,128)S(1)} %copy-done.5, s32[2048]{0:T(1024)S(1)} %le.57), kind=kOutput, calls=%fused_computation.18 | convolution fusion | flops 547356672 | bytes 9728000 | tf_op jit(solution)/shard_map/cond/branch_1_fun/hrn,hrd->nhd/dot_general | solution.py:138
  144.0 1.2 copy.58
  145.1 3.5 %all-to-all-start.3 = ((bf16[2,256,8,128]{3,2,0,1:T(8,128)(2,1)}), bf16[2,256,8,128]{3,2,0,1:T(8,128)(2,1)S(1)}, u32[]{:S(2)}, u32[]{:S(2)}) async-start(bf16[2,256,8,128]{3,2,0,1:T(8,128)(2,1)} %copy.58), calls=%async_computation.3 | async-start | bytes 2097152 | tf_op jit(solution)/shard_map/all_to_all | solution.py:124
  148.7 59.2 %reduce-scatter.2.cloned.1.call-done = bf16[64,2,256]{2,0,1:T(8,128)(2,1)} async-done(((bf16[512,2,256]{2,0,1:T(8,128)(2,1)}), bf16[64,2,256]{2,0,1:T(8,128)(2,1)}) %reduce-scatter.2.cloned.1.call-update) | async-done | bytes 65552 | tf_op jit(solution)/shard_map/reduce_scatter | solution.py:157
  208.6 3.4 %collective-permute-start.1 = (bf16[1,2,256]{2,0,1:T(2,128)(2,1)S(1)}, bf16[1,2,256]{2,0,1:T(2,128)(2,1)S(1)}, u32[]{:S(2)}, u32[]{:S(2)}) collective-permute-start(bf16[1,2,256]{2,0,1:T(2,128)(2,1)S(1)} %slice.52), channel_id=1, source_target_pairs={{0,4},{4,8},{8,12},{12,16},{16,20},{20,24},{24,28},{1,5},{5,9},{9,... | collective-permute-start | bytes 3080 | tf_op jit(solution)/shard_map/ppermute | solution.py:14
  212.1 2.9 %collective-permute-done.1 = bf16[1,2,256]{2,0,1:T(2,128)(2,1)S(1)} collective-permute-done((bf16[1,2,256]{2,0,1:T(2,128)(2,1)S(1)}, bf16[1,2,256]{2,0,1:T(2,128)(2,1)S(1)}, u32[]{:S(2)}, u32[]{:S(2)}) %collective-permute-start.1) | collective-permute-done | bytes 1056 | tf_op jit(solution)/shard_map/ppermute | solution.py:14
  217.0 3.3 %all-to-all-start.6 = ((bf16[2,256,128]{2,0,1:T(2,128)(2,1)}), bf16[2,256,128]{2,0,1:T(2,128)(2,1)S(1)}, u32[]{:S(2)}, u32[]{:S(2)}) async-start(bf16[2,256,128]{2,0,1:T(2,128)(2,1)} %copy.66), calls=%async_computation.7 | async-start | bytes 262144 | tf_op jit(solution)/shard_map/all_to_all | solution.py:185
  220.3 1.2 copy.60
  222.3 2.6 %all-to-all-done.6 = bf16[2,256,128]{2,0,1:T(2,128)(2,1)S(1)} async-done(((bf16[2,256,128]{2,0,1:T(2,128)(2,1)}), bf16[2,256,128]{2,0,1:T(2,128)(2,1)S(1)}, u32[]{:S(2)}, u32[]{:S(2)}) %all-to-all-start.6) | async-done | bytes 131104 | tf_op jit(solution)/shard_map/all_to_all | solution.py:185
  224.9 3.3 %all-to-all-start.5 = ((bf16[2,256,128]{2,0,1:T(2,128)(2,1)}), bf16[2,256,128]{2,0,1:T(2,128)(2,1)S(1)}, u32[]{:S(2)}, u32[]{:S(2)}) async-start(bf16[2,256,128]{2,0,1:T(2,128)(2,1)} %copy.64), calls=%async_computation.6 | async-start | bytes 262144 | tf_op jit(solution)/shard_map/all_to_all | solution.py:178
  229.1 3.8 %all-to-all-done.5 = bf16[2,256,128]{2,0,1:T(2,128)(2,1)S(1)} async-done(((bf16[2,256,128]{2,0,1:T(2,128)(2,1)}), bf16[2,256,128]{2,0,1:T(2,128)(2,1)S(1)}, u32[]{:S(2)}, u32[]{:S(2)}) %all-to-all-start.5) | async-done | bytes 131104 | tf_op jit(solution)/shard_map/all_to_all | solution.py:178
  (62 shorter events, 12.8 us)
Async XLA Ops:
  7.2 7.9 %all-to-all-start = ((bf16[8,64,128]{2,1,0:T(8,128)(2,1)}), bf16[8,64,128]{2,1,0:T(8,128)(2,1)S(1)}, u32[]{:S(2)}, u32[]{:S(2)}) async-start(bf16[8,64,128]{2,1,0:T(8,128)(2,1)} %param.11), calls=%async_computation | async-start | bytes 262144 | tf_op jit(solution)/shard_map/all_to_all | solution.py:25
  15.1 7.9 %all-to-all-start.1 = ((bf16[8,64,128]{2,1,0:T(8,128)(2,1)}), bf16[8,64,128]{2,1,0:T(8,128)(2,1)S(1)}, u32[]{:S(2)}, u32[]{:S(2)}) async-start(bf16[8,64,128]{2,1,0:T(8,128)(2,1)} %param.12), calls=%async_computation.1 | async-start | bytes 262144 | tf_op jit(solution)/shard_map/all_to_all | solution.py:26
  23.0 18.0 %all-to-all-start.2 = ((bf16[8,64,8,128]{3,2,1,0:T(8,128)(2,1)}), bf16[8,64,8,128]{3,2,1,0:T(8,128)(2,1)S(1)}, u32[]{:S(2)}, u32[]{:S(2)}) async-start(bf16[8,64,8,128]{3,2,1,0:T(8,128)(2,1)} %param.13), calls=%async_computation.2 | async-start | bytes 2097152 | tf_op jit(solution)/shard_map/all_to_all | solution.py:27
  41.0 80.1 %all-to-all-start.4 = ((bf16[8,64,8,128]{3,2,1,0:T(8,128)(2,1)}), bf16[8,64,8,128]{3,2,1,0:T(8,128)(2,1)}, u32[]{:S(2)}, u32[]{:S(2)}) async-start(bf16[8,64,8,128]{3,2,1,0:T(8,128)(2,1)} %param.14), calls=%async_computation.4 | async-start | bytes 2097152 | tf_op jit(solution)/shard_map/all_to_all | solution.py:28
  45.3 162.7 %reduce-scatter.2.cloned.1.call-start = ((), (), s32[]{:S(2)}) async-start(), calls=%async_computation.8 | async-start | bytes 589824 | tf_op jit(solution)/shard_map/reduce_scatter | solution.py:157
  45.5 5.5 %collective-permute-start = (f32[1,2,256]{2,0,1:T(1,128)S(1)}, f32[1,2,256]{2,0,1:T(1,128)S(1)}, u32[]{:S(2)}, u32[]{:S(2)}) collective-permute-start(f32[1,2,256]{2,0,1:T(1,128)S(1)} %slice.50), channel_id=1, source_target_pairs={{4,0},{8,4},{12,8},{16,12},{20,16},{24,20},{28,24},{5,1},{9,5},{13... | collective-permute-start | bytes 6152 | tf_op jit(solution)/shard_map/ppermute | solution.py:14
  111.0 6.5 %copy-start.4 = (bf16[512,2,256]{2,0,1:T(8,128)(2,1)}, bf16[512,2,256]{2,0,1:T(8,128)(2,1)S(1)}, u32[]{:S(2)}) copy-start(bf16[512,2,256]{2,0,1:T(8,128)(2,1)S(1)} %all_gather.7) | copy-start | bytes 1572868
  111.0 6.4 %copy-start = (bf16[2,4,64,8,128]{4,3,2,1,0:T(8,128)(2,1)}, bf16[2,4,64,8,128]{4,3,2,1,0:T(8,128)(2,1)S(1)}, u32[]{:S(2)}) copy-start(bf16[2,4,64,8,128]{4,3,2,1,0:T(8,128)(2,1)S(1)} %copy.57) | copy-start | bytes 3145732
  122.1 8.2 %copy-start.5 = (s32[2,512]{1,0:T(2,128)S(1)}, s32[2,512]{1,0:T(2,128)}, u32[]{:S(2)}) copy-start(s32[2,512]{1,0:T(2,128)} %le.55) | copy-start | bytes 12292 | tf_op jit(solution)/shard_map/cond
  123.4 1.0 copy-start.2
  124.4 5.9 %copy-start.1 = (bf16[2,2048,128]{2,1,0:T(8,128)(2,1)S(1)}, bf16[2,2048,128]{2,1,0:T(8,128)(2,1)}, u32[]{:S(2)}) copy-start(bf16[2,2048,128]{2,1,0:T(8,128)(2,1)} %get-tuple-element.117) | copy-start | bytes 3145732 | tf_op jit(solution)/shard_map/cond
  124.4 5.9 %copy-start.3 = (bf16[2,4,64,8,128]{4,3,2,1,0:T(8,128)(2,1)S(1)}, bf16[2,4,64,8,128]{4,3,2,1,0:T(8,128)(2,1)}, u32[]{:S(2)}) copy-start(bf16[2,4,64,8,128]{4,3,2,1,0:T(8,128)(2,1)} %copy-done.2) | copy-start | bytes 3145732 | tf_op jit(solution)/shard_map/cond
  145.1 71.9 %all-to-all-start.3 = ((bf16[2,256,8,128]{3,2,0,1:T(8,128)(2,1)}), bf16[2,256,8,128]{3,2,0,1:T(8,128)(2,1)S(1)}, u32[]{:S(2)}, u32[]{:S(2)}) async-start(bf16[2,256,8,128]{3,2,0,1:T(8,128)(2,1)} %copy.58), calls=%async_computation.3 | async-start | bytes 2097152 | tf_op jit(solution)/shard_map/all_to_all | solution.py:124
  208.6 6.4 %collective-permute-start.1 = (bf16[1,2,256]{2,0,1:T(2,128)(2,1)S(1)}, bf16[1,2,256]{2,0,1:T(2,128)(2,1)S(1)}, u32[]{:S(2)}, u32[]{:S(2)}) collective-permute-start(bf16[1,2,256]{2,0,1:T(2,128)(2,1)S(1)} %slice.52), channel_id=1, source_target_pairs={{0,4},{4,8},{8,12},{12,16},{16,20},{20,24},{24,28},{1,5},{5,9},{9,... | collective-permute-start | bytes 3080 | tf_op jit(solution)/shard_map/ppermute | solution.py:14
  217.0 7.9 %all-to-all-start.6 = ((bf16[2,256,128]{2,0,1:T(2,128)(2,1)}), bf16[2,256,128]{2,0,1:T(2,128)(2,1)S(1)}, u32[]{:S(2)}, u32[]{:S(2)}) async-start(bf16[2,256,128]{2,0,1:T(2,128)(2,1)} %copy.66), calls=%async_computation.7 | async-start | bytes 262144 | tf_op jit(solution)/shard_map/all_to_all | solution.py:185
  224.9 7.9 %all-to-all-start.5 = ((bf16[2,256,128]{2,0,1:T(2,128)(2,1)}), bf16[2,256,128]{2,0,1:T(2,128)(2,1)S(1)}, u32[]{:S(2)}, u32[]{:S(2)}) async-start(bf16[2,256,128]{2,0,1:T(2,128)(2,1)} %copy.64), calls=%async_computation.6 | async-start | bytes 262144 | tf_op jit(solution)/shard_map/all_to_all | solution.py:178
Sparse Core Ops, SparseCore 0:
  144.1 63.8 reduce-scatter.1
where the time goes:
time: 242 us; the launch traced here: 241 us
  waiting for transfers between devices  90.6 us (37%)
  blocking collectives  59.9 us (25%)
  starting transfers between devices  31.3 us (13%)
  matrix products  24.4 us (10%)
  between operations  14.9 us (6%)
  local copies, waits for them, and re-layouts  11 us (5%)
  other arithmetic  8.1 us (3%)
    reduce_scatter x1, waiting for transfers between devices, per_device(): lax.psum_scatter(partials.astype(jnp.bfloat16), 'ctx', scatter_dimension=...  59.2 us
    all_gather x1, blocking collectives, per_device(): pair_block = lax.all_gather(slot_pairs, 'ctx', axis=0, tiled=True)  31.5 us
    all_gather x1, blocking collectives, per_device(): lax.all_gather(slot_pairs[:, :, :head_dim], 'ctx', axis=0, tiled=True)  28.4 us
    all_to_all x1, waiting for transfers between devices, per_device(): lax.all_to_all(queries, 'head', split_axis=0, concat_axis=1, tiled=True)  13.4 us
    dot_general x2, matrix products, block_scores(): jnp.einsum('hrd,nhd->hrn', query_rows, key_block, preferred_element_type=...  7.21 us
    dot_general x1, matrix products, grad_advance(): jnp.einsum('hrn,hrd->nhd', dscores, query_rows, preferred_element_type=jn...  6.96 us
    ppermute x2, starting transfers between devices, from_behind(): lax.ppermute(value, axis, [(source, source + steps) for source in range(i...  6.64 us
    dot_general x1, matrix products, grad_advance(): jnp.einsum('hrn,hrd->nhd', weights_low, grad_rows, preferred_element_type...  5.63 us
  transfers between devices with their start and end apart: 10, of which 8 were waited for; matrix products, arithmetic and copies ran while one was open for 8% of the time, Pallas kernels for 0%

commit v1 on v0

--- a/solution.py
+++ b/solution.py
@@ -8,6 +8,18 @@
 neg_big = -1e30
 
 
+def rotated_exchange(x, axis, split, join):
+    ways, here = (lax.axis_size(axis), lax.axis_index(axis))
+    width = x.shape[split] // ways
+    turned = jnp.roll(x, -here * width, axis=split)
+    got = [lax.slice_in_dim(turned, 0, width, axis=split)]
+    for far in range(1, ways):
+        sent = lax.slice_in_dim(turned, far * width, (far + 1) * width, axis=split)
+        got.append(lax.ppermute(sent, axis, [(d, (d + far) % ways) for d in range(ways)]))
+    line = jnp.concatenate(got[::-1], axis=join)
+    return jnp.roll(line, (here + 1) * got[0].shape[join], axis=join)
+
+
 def from_behind(value, axis, steps):
     count = lax.axis_size(axis)
     initial, last = (max(0, -steps), min(count, count - steps))
@@ -23,7 +35,7 @@
 def per_device(token_keys, token_values, queries, out_grad, slot_ids):
     keys_here, values_here, query_here, grad_here = (
         lax.all_to_all(token_keys, "head", split_axis=0, concat_axis=1, tiled=True),
-        lax.all_to_all(token_values, "head", split_axis=0, concat_axis=1, tiled=True),
+        rotated_exchange(token_values, "head", 0, 1),
         lax.all_to_all(queries, "head", split_axis=0, concat_axis=1, tiled=True),
         lax.all_to_all(out_grad, "head", split_axis=0, concat_axis=1, tiled=True),
     )

time: 242 us -> 237 us (0.979)
  waiting for transfers between devices: 90.6 us -> 84.3 us
    all_to_all x1 -> x0, waiting for transfers between devices: 4.58 us -> none  [per_device(): lax.all_to_all(token_values, 'head', split_axis=0, concat_axis=1, tiled=T...]
    ppermute x0 -> x3, starting transfers between devices: none -> 3.44 us  [rotated_exchange(): lax.ppermute(sent, axis, [(d, (d + far) % ways) for d in range(ways)])]
    all_to_all x1 -> x0, starting transfers between devices: 3.33 us -> none  [per_device(): lax.all_to_all(token_values, 'head', split_axis=0, concat_axis=1, tiled=T...]
    all_to_all x1, waiting for transfers between devices: 2.63 us -> 0.01 us  [per_device(): lax.all_to_all(token_keys, 'head', split_axis=0, concat_axis=1, tiled=True)]
  transfers between devices with their start and end apart: 10 -> 12, of which waited for: 8 -> 6; matrix products, arithmetic and copies ran while one was open for 8% -> 9% of each run, Pallas kernels for 0% -> 0%
where the time goes in v1:
time: 237 us; the launch traced here: 235 us
  waiting for transfers between devices  84.3 us (36%)
  blocking collectives  59.9 us (25%)
  starting transfers between devices  31.4 us (13%)
  matrix products  24.5 us (10%)
  between operations  15 us (6%)
  local copies, waits for them, and re-layouts  11.1 us (5%)
  other arithmetic  9.07 us (4%)
    reduce_scatter x1, waiting for transfers between devices, per_device(): lax.psum_scatter(partials.astype(jnp.bfloat16), 'ctx', scatter_dimension=...  59.2 us
    all_gather x1, blocking collectives, per_device(): pair_block = lax.all_gather(slot_pairs, 'ctx', axis=0, tiled=True)  31.5 us
    all_gather x1, blocking collectives, per_device(): lax.all_gather(slot_pairs[:, :, :head_dim], 'ctx', axis=0, tiled=True)  28.4 us
    all_to_all x1, waiting for transfers between devices, per_device(): lax.all_to_all(queries, 'head', split_axis=0, concat_axis=1, tiled=True)  14.3 us
    dot_general x2, matrix products, block_scores(): jnp.einsum('hrd,nhd->hrn', query_rows, key_block, preferred_element_type=...  7.23 us
    dot_general x1, matrix products, grad_advance(): jnp.einsum('hrn,hrd->nhd', dscores, query_rows, preferred_element_type=jn...  6.96 us
    ppermute x2, starting transfers between devices, from_behind(): lax.ppermute(value, axis, [(source, source + steps) for source in range(i...  6.64 us
    dot_general x1, matrix products, grad_advance(): jnp.einsum('hrn,hrd->nhd', weights_low, grad_rows, preferred_element_type...  5.63 us
  transfers between devices with their start and end apart: 12, of which 6 were waited for; matrix products, arithmetic and copies ran while one was open for 9% of the time, Pallas kernels for 0%

profile of v1, /device:TPU:8, one launch (start us, length us, event | category | flops | bytes accessed | tf_op | source)
XLA Modules:
  0.0 235.4 jit_solution(8510182175297179998)
XLA Ops:
  7.2 3.3 %all-to-all-start = ((bf16[8,64,128]{2,1,0:T(8,128)(2,1)}), bf16[8,64,128]{2,1,0:T(8,128)(2,1)S(1)}, u32[]{:S(2)}, u32[]{:S(2)}) async-start(bf16[8,64,128]{2,1,0:T(8,128)(2,1)} %param.11), calls=%async_computation | async-start | bytes 262144 | tf_op jit(solution)/shard_map/all_to_all | solution.py:37
  12.0 1.7 collective-permute-start.1
  13.7 1.3 collective-permute-start
  18.0 3.5 %all-to-all-start.1 = ((bf16[8,64,8,128]{3,2,1,0:T(8,128)(2,1)}), bf16[8,64,8,128]{3,2,1,0:T(8,128)(2,1)S(1)}, u32[]{:S(2)}, u32[]{:S(2)}) async-start(bf16[8,64,8,128]{3,2,1,0:T(8,128)(2,1)} %param.13), calls=%async_computation.1 | async-start | bytes 2097152 | tf_op jit(solution)/shard_map/all_to_all | solution.py:39
  21.7 14.3 %all-to-all-done.1 = bf16[8,64,8,128]{3,2,1,0:T(8,128)(2,1)S(1)} async-done(((bf16[8,64,8,128]{3,2,1,0:T(8,128)(2,1)}), bf16[8,64,8,128]{3,2,1,0:T(8,128)(2,1)S(1)}, u32[]{:S(2)}, u32[]{:S(2)}) %all-to-all-start.1) | async-done | bytes 1048608 | tf_op jit(solution)/shard_map/all_to_all | solution.py:39
  36.0 4.3 %all-to-all-start.3 = ((bf16[8,64,8,128]{3,2,1,0:T(8,128)(2,1)}), bf16[8,64,8,128]{3,2,1,0:T(8,128)(2,1)}, u32[]{:S(2)}, u32[]{:S(2)}) async-start(bf16[8,64,8,128]{3,2,1,0:T(8,128)(2,1)} %param.14), calls=%async_computation.3 | async-start | bytes 2097152 | tf_op jit(solution)/shard_map/all_to_all | solution.py:40
  40.5 3.3 %collective-permute-start.3 = (f32[1,2,256]{2,0,1:T(1,128)S(1)}, f32[1,2,256]{2,0,1:T(1,128)S(1)}, u32[]{:S(2)}, u32[]{:S(2)}) collective-permute-start(f32[1,2,256]{2,0,1:T(1,128)S(1)} %slice.70), channel_id=1, source_target_pairs={{4,0},{8,4},{12,8},{16,12},{20,16},{24,20},{28,24},{5,1},{9,5},{13... | collective-permute-start | bytes 6152 | tf_op jit(solution)/shard_map/ppermute | solution.py:26
  44.5 1.5 collective-permute-done.3
  46.1 28.4 %all_gather.8 = bf16[512,2,128]{2,0,1:T(8,128)(2,1)S(1)} all-gather(bf16[64,2,128]{2,0,1:T(8,128)(2,1)S(1)} %slice.71), channel_id=1, replica_groups=mesh['ctx'=8,'head'=4] {'ctx'}, dimensions={0}, use_global_device_ids=true | all-gather | bytes 294912 | tf_op jit(solution)/shard_map/all_gather | solution.py:104
  74.5 31.5 %all_gather.7 = bf16[512,2,256]{2,0,1:T(8,128)(2,1)S(1)} all-gather(bf16[64,2,256]{2,0,1:T(8,128)(2,1)S(1)} %fusion.32), channel_id=1, replica_groups=mesh['ctx'=8,'head'=4] {'ctx'}, dimensions={0}, use_global_device_ids=true | all-gather | bytes 589824 | tf_op jit(solution)/shard_map/all_gather | solution.py:123
  106.1 4.9 %conditional.3 = (f32[2,2048]{1,0:T(2,128)}, f32[2,2048]{1,0:T(2,128)S(1)}) conditional(s32[]{:T(128)} %convert_element_type.72, () %tuple.34, (s32[2,8,64]{2,1,0:T(8,128)S(1)}, s32[256,8]{1,0:T(8,128)S(1)}, bf16[2,2048,128]{2,1,0:T(8,128)(2,1)S(1)}, bf16[512,2,128]{2,0,1:T(8,128)(2,1)S(1)}) %tuple.58), branch_computations={%region_2.3_spmd, %region_3.6_spmd} | conditional | flops 555741184 | bytes 18251792 | solution.py:113
  106.3 1.3 fusion
  108.3 2.7 %fusion.1 = f32[2,2048]{1,0:T(2,128)S(1)} fusion(f32[2,2048,512]{1,2,0:T(8,128)S(1)} %get-tuple-element.122, f32[2,2048]{1,0:T(2,128)} %broadcast_maximum_fusion, s32[2048]{0:T(1024)S(1)} %le.37, s32[2,512]{1,0:T(2,128)S(1)} %le.35), kind=kLoop, calls=%fused_computation.3 | loop fusion | flops 10481664 | bytes 8433664 | tf_op jit(solution)/shard_map/cond/branch_1_fun/reduce_sum | solution.py:110
  111.1 1.3 add.125
  112.4 3.5 %conditional.4 = (bf16[2,2048,128]{2,1,0:T(8,128)(2,1)S(1)}) conditional(s32[]{:T(128)} %convert_element_type.72, () %tuple.33, (s32[2,8,64]{2,1,0:T(8,128)S(1)}, s32[256,8]{1,0:T(8,128)S(1)}, bf16[512,2,256]{2,0,1:T(8,128)(2,1)S(1)}, bf16[2,2048,128]{2,1,0:T(8,128)(2,1)S(1)}, f32[2,2048]{1,0:T(2,128)}) %tuple.59), branch_computations={%region_6.7_spmd, %region_7.8_spmd} | conditional | flops 1084227584 | bytes 2674696 | solution.py:134
  112.6 3.3 %fusion.2 = bf16[2,2048,128]{2,1,0:T(8,128)(2,1)S(1)} fusion(bf16[2,2048,128]{2,1,0:T(8,128)(2,1)S(1)} %get-tuple-element.67, f32[2,2048]{1,0:T(2,128)} %get-tuple-element.69, s32[2,512]{1,0:T(2,128)S(1)} %le.50, s32[2048]{0:T(1024)S(1)} %le.52, bf16[512,2,256]{2,0,1:T(8,128)(2,1)S(1)} %get-tuple-element.68), kind=kOutput, calls=%fused_computation.6 | convolution fusion | flops 1084227584 | bytes 2650112 | tf_op jit(solution)/shard_map/cond/branch_1_fun/hrn,nhd->hrd/dot_general | solution.py:127
  116.1 21.8 %conditional.5 = (bf16[512,2,256]{0,2,1:T(8,128)(2,1)S(1)}) conditional(s32[]{:T(128)} %convert_element_type.72, () %tuple.37, (s32[2,8,64]{2,1,0:T(8,128)S(1)}, s32[256,8]{1,0:T(8,128)S(1)}, bf16[512,2,256]{2,0,1:T(8,128)(2,1)}, bf16[2,2048,128]{2,1,0:T(8,128)(2,1)}, f32[2,2048]{1,0:T(2,128)}, /*index=5*/bf16[2,4,64,8,128]{4,3,2,0,1:T(8,128)(2,1)}, ...), branch_computations={%region_8.9_spmd, %region_9.11_spmd} | conditional | flops 2175528960 | bytes 49414264 | solution.py:166
  117.1 1.3 copy.57
  119.4 5.9 %fusion.20 = f32[2,2048,512]{2,1,0:T(8,128)} fusion(bf16[2,2048,128]{2,1,0:T(8,128)(2,1)} %get-tuple-element.117, bf16[512,2,256]{2,0,1:T(8,128)(2,1)} %get-tuple-element.73), kind=kOutput, calls=%fused_computation.23 | convolution fusion | flops 536870912 | bytes 9699328 | tf_op jit(solution)/shard_map/cond/branch_1_fun/hrd,nhd->hrn/dot_general | solution.py:88
  125.3 7.0 %fusion.17 = bf16[512,2,128]{0,2,1:T(8,128)(2,1)S(1)} fusion(bf16[2,2048,128]{2,1,0:T(8,128)(2,1)S(1)} %copy-done.1, f32[2,2048,512]{2,1,0:T(8,128)} %fusion.20, bf16[2,2048,128]{2,1,0:T(8,128)(2,1)S(1)} %bitcast.53, f32[2,2048]{1,0:T(2,128)S(1)} %multiply_reduce_fusion, f32[2,2048]{1,0:T(2,128)} %get-tuple-element.74, s32[2,512]{1,0:T(2,128)S(1)} %copy-done.5, ...), kind=kOutput, calls=%fused_computation.20 | convolution fusion | flops 1088684032 | bytes 11055104 | tf_op jit(solution)/shard_map/cond/branch_1_fun/hrn,hrd->nhd/dot_general | solution.py:161
  132.2 5.6 %fusion.13 = bf16[512,2,128]{0,2,1:T(8,128)(2,1)S(1)} fusion(bf16[2,2048,128]{2,1,0:T(8,128)(2,1)S(1)} %bitcast.54, f32[2,2048,512]{2,1,0:T(8,128)} %fusion.20, f32[2,2048]{1,0:T(2,128)} %get-tuple-element.74, s32[2,512]{1,0:T(2,128)S(1)} %copy-done.5, s32[2048]{0:T(1024)S(1)} %le.57), kind=kOutput, calls=%fused_computation.18 | convolution fusion | flops 547356672 | bytes 9728000 | tf_op jit(solution)/shard_map/cond/branch_1_fun/hrn,hrd->nhd/dot_general | solution.py:150
  138.9 1.2 copy.53
  140.1 3.5 %all-to-all-start.2 = ((bf16[2,256,8,128]{3,2,0,1:T(8,128)(2,1)}), bf16[2,256,8,128]{3,2,0,1:T(8,128)(2,1)S(1)}, u32[]{:S(2)}, u32[]{:S(2)}) async-start(bf16[2,256,8,128]{3,2,0,1:T(8,128)(2,1)} %copy.53), calls=%async_computation.2 | async-start | bytes 2097152 | tf_op jit(solution)/shard_map/all_to_all | solution.py:136
  143.7 59.2 %reduce-scatter.2.cloned.1.call-done = bf16[64,2,256]{2,0,1:T(8,128)(2,1)} async-done(((bf16[512,2,256]{2,0,1:T(8,128)(2,1)}), bf16[64,2,256]{2,0,1:T(8,128)(2,1)}) %reduce-scatter.2.cloned.1.call-update) | async-done | bytes 65552 | tf_op jit(solution)/shard_map/reduce_scatter | solution.py:169
  203.6 3.4 %collective-permute-start.4 = (bf16[1,2,256]{2,0,1:T(2,128)(2,1)S(1)}, bf16[1,2,256]{2,0,1:T(2,128)(2,1)S(1)}, u32[]{:S(2)}, u32[]{:S(2)}) collective-permute-start(bf16[1,2,256]{2,0,1:T(2,128)(2,1)S(1)} %slice.72), channel_id=1, source_target_pairs={{0,4},{4,8},{8,12},{12,16},{16,20},{20,24},{24,28},{1,5},{5,9},{9,... | collective-permute-start | bytes 3080 | tf_op jit(solution)/shard_map/ppermute | solution.py:26
  207.0 2.9 %collective-permute-done.4 = bf16[1,2,256]{2,0,1:T(2,128)(2,1)S(1)} collective-permute-done((bf16[1,2,256]{2,0,1:T(2,128)(2,1)S(1)}, bf16[1,2,256]{2,0,1:T(2,128)(2,1)S(1)}, u32[]{:S(2)}, u32[]{:S(2)}) %collective-permute-start.4) | collective-permute-done | bytes 1056 | tf_op jit(solution)/shard_map/ppermute | solution.py:26
  209.9 1.1 fusion.26
  211.9 3.3 %all-to-all-start.5 = ((bf16[2,256,128]{2,0,1:T(2,128)(2,1)}), bf16[2,256,128]{2,0,1:T(2,128)(2,1)S(1)}, u32[]{:S(2)}, u32[]{:S(2)}) async-start(bf16[2,256,128]{2,0,1:T(2,128)(2,1)} %copy.61), calls=%async_computation.6 | async-start | bytes 262144 | tf_op jit(solution)/shard_map/all_to_all | solution.py:197
  215.2 1.2 copy.55
  217.2 2.6 %all-to-all-done.5 = bf16[2,256,128]{2,0,1:T(2,128)(2,1)S(1)} async-done(((bf16[2,256,128]{2,0,1:T(2,128)(2,1)}), bf16[2,256,128]{2,0,1:T(2,128)(2,1)S(1)}, u32[]{:S(2)}, u32[]{:S(2)}) %all-to-all-start.5) | async-done | bytes 131104 | tf_op jit(solution)/shard_map/all_to_all | solution.py:197
  219.8 3.3 %all-to-all-start.4 = ((bf16[2,256,128]{2,0,1:T(2,128)(2,1)}), bf16[2,256,128]{2,0,1:T(2,128)(2,1)S(1)}, u32[]{:S(2)}, u32[]{:S(2)}) async-start(bf16[2,256,128]{2,0,1:T(2,128)(2,1)} %copy.59), calls=%async_computation.5 | async-start | bytes 262144 | tf_op jit(solution)/shard_map/all_to_all | solution.py:190
  224.0 3.8 %all-to-all-done.4 = bf16[2,256,128]{2,0,1:T(2,128)(2,1)S(1)} async-done(((bf16[2,256,128]{2,0,1:T(2,128)(2,1)}), bf16[2,256,128]{2,0,1:T(2,128)(2,1)S(1)}, u32[]{:S(2)}, u32[]{:S(2)}) %all-to-all-start.4) | async-done | bytes 131104 | tf_op jit(solution)/shard_map/all_to_all | solution.py:190
  (76 shorter events, 13.2 us)
Async XLA Ops:
  7.2 10.8 %all-to-all-start = ((bf16[8,64,128]{2,1,0:T(8,128)(2,1)}), bf16[8,64,128]{2,1,0:T(8,128)(2,1)S(1)}, u32[]{:S(2)}, u32[]{:S(2)}) async-start(bf16[8,64,128]{2,1,0:T(8,128)(2,1)} %param.11), calls=%async_computation | async-start | bytes 262144 | tf_op jit(solution)/shard_map/all_to_all | solution.py:37
  11.5 6.5 %collective-permute-start.2 = (bf16[2,64,128]{2,1,0:T(8,128)(2,1)S(1)}, bf16[2,64,128]{2,1,0:T(8,128)(2,1)S(1)}, u32[]{:S(2)}, u32[]{:S(2)}) collective-permute-start(bf16[2,64,128]{2,1,0:T(8,128)(2,1)S(1)} %get-tuple-element.125), channel_id=1, source_target_pairs={{0,1},{1,2},{2,3},{3,0},{4,5},{5,6},{6,7},{7,4},{8,9},{9,10},{10,1... | collective-permute-start | bytes 98312 | tf_op jit(solution)/shard_map/ppermute | solution.py:18
  12.0 6.0 %collective-permute-start.1 = (bf16[2,64,128]{2,1,0:T(8,128)(2,1)S(1)}, bf16[2,64,128]{2,1,0:T(8,128)(2,1)S(1)}, u32[]{:S(2)}, u32[]{:S(2)}) collective-permute-start(bf16[2,64,128]{2,1,0:T(8,128)(2,1)S(1)} %get-tuple-element.126), channel_id=1, source_target_pairs={{0,2},{1,3},{2,0},{3,1},{4,6},{5,7},{6,4},{7,5},{8,10},{9,11},{10,... | collective-permute-start | bytes 98312 | tf_op jit(solution)/shard_map/ppermute | solution.py:18
  13.7 4.3 %collective-permute-start = (bf16[2,64,128]{2,1,0:T(8,128)(2,1)S(1)}, bf16[2,64,128]{2,1,0:T(8,128)(2,1)S(1)}, u32[]{:S(2)}, u32[]{:S(2)}) collective-permute-start(bf16[2,64,128]{2,1,0:T(8,128)(2,1)S(1)} %get-tuple-element.127), channel_id=1, source_target_pairs={{0,3},{1,0},{2,1},{3,2},{4,7},{5,4},{6,5},{7,6},{8,11},{9,8},{10,9... | collective-permute-start | bytes 98312 | tf_op jit(solution)/shard_map/ppermute | solution.py:18
  18.0 18.0 %all-to-all-start.1 = ((bf16[8,64,8,128]{3,2,1,0:T(8,128)(2,1)}), bf16[8,64,8,128]{3,2,1,0:T(8,128)(2,1)S(1)}, u32[]{:S(2)}, u32[]{:S(2)}) async-start(bf16[8,64,8,128]{3,2,1,0:T(8,128)(2,1)} %param.13), calls=%async_computation.1 | async-start | bytes 2097152 | tf_op jit(solution)/shard_map/all_to_all | solution.py:39
  36.0 80.1 %all-to-all-start.3 = ((bf16[8,64,8,128]{3,2,1,0:T(8,128)(2,1)}), bf16[8,64,8,128]{3,2,1,0:T(8,128)(2,1)}, u32[]{:S(2)}, u32[]{:S(2)}) async-start(bf16[8,64,8,128]{3,2,1,0:T(8,128)(2,1)} %param.14), calls=%async_computation.3 | async-start | bytes 2097152 | tf_op jit(solution)/shard_map/all_to_all | solution.py:40
  40.3 162.6 %reduce-scatter.2.cloned.1.call-start = ((), (), s32[]{:S(2)}) async-start(), calls=%async_computation.7 | async-start | bytes 589824 | tf_op jit(solution)/shard_map/reduce_scatter | solution.py:169
  40.5 5.5 %collective-permute-start.3 = (f32[1,2,256]{2,0,1:T(1,128)S(1)}, f32[1,2,256]{2,0,1:T(1,128)S(1)}, u32[]{:S(2)}, u32[]{:S(2)}) collective-permute-start(f32[1,2,256]{2,0,1:T(1,128)S(1)} %slice.70), channel_id=1, source_target_pairs={{4,0},{8,4},{12,8},{16,12},{20,16},{24,20},{28,24},{5,1},{9,5},{13... | collective-permute-start | bytes 6152 | tf_op jit(solution)/shard_map/ppermute | solution.py:26
  105.9 6.5 %copy-start.4 = (bf16[512,2,256]{2,0,1:T(8,128)(2,1)}, bf16[512,2,256]{2,0,1:T(8,128)(2,1)S(1)}, u32[]{:S(2)}) copy-start(bf16[512,2,256]{2,0,1:T(8,128)(2,1)S(1)} %all_gather.7) | copy-start | bytes 1572868
  106.0 6.4 %copy-start = (bf16[2,4,64,8,128]{4,3,2,1,0:T(8,128)(2,1)}, bf16[2,4,64,8,128]{4,3,2,1,0:T(8,128)(2,1)S(1)}, u32[]{:S(2)}) copy-start(bf16[2,4,64,8,128]{4,3,2,1,0:T(8,128)(2,1)S(1)} %copy.52) | copy-start | bytes 3145732
  117.1 8.2 %copy-start.5 = (s32[2,512]{1,0:T(2,128)S(1)}, s32[2,512]{1,0:T(2,128)}, u32[]{:S(2)}) copy-start(s32[2,512]{1,0:T(2,128)} %le.55) | copy-start | bytes 12292 | tf_op jit(solution)/shard_map/cond
  118.4 1.0 copy-start.2
  119.3 5.9 %copy-start.1 = (bf16[2,2048,128]{2,1,0:T(8,128)(2,1)S(1)}, bf16[2,2048,128]{2,1,0:T(8,128)(2,1)}, u32[]{:S(2)}) copy-start(bf16[2,2048,128]{2,1,0:T(8,128)(2,1)} %get-tuple-element.117) | copy-start | bytes 3145732 | tf_op jit(solution)/shard_map/cond
  119.4 5.9 %copy-start.3 = (bf16[2,4,64,8,128]{4,3,2,1,0:T(8,128)(2,1)S(1)}, bf16[2,4,64,8,128]{4,3,2,1,0:T(8,128)(2,1)}, u32[]{:S(2)}) copy-start(bf16[2,4,64,8,128]{4,3,2,1,0:T(8,128)(2,1)} %copy-done.2) | copy-start | bytes 3145732 | tf_op jit(solution)/shard_map/cond
  140.1 71.8 %all-to-all-start.2 = ((bf16[2,256,8,128]{3,2,0,1:T(8,128)(2,1)}), bf16[2,256,8,128]{3,2,0,1:T(8,128)(2,1)S(1)}, u32[]{:S(2)}, u32[]{:S(2)}) async-start(bf16[2,256,8,128]{3,2,0,1:T(8,128)(2,1)} %copy.53), calls=%async_computation.2 | async-start | bytes 2097152 | tf_op jit(solution)/shard_map/all_to_all | solution.py:136
  203.6 6.4 %collective-permute-start.4 = (bf16[1,2,256]{2,0,1:T(2,128)(2,1)S(1)}, bf16[1,2,256]{2,0,1:T(2,128)(2,1)S(1)}, u32[]{:S(2)}, u32[]{:S(2)}) collective-permute-start(bf16[1,2,256]{2,0,1:T(2,128)(2,1)S(1)} %slice.72), channel_id=1, source_target_pairs={{0,4},{4,8},{8,12},{12,16},{16,20},{20,24},{24,28},{1,5},{5,9},{9,... | collective-permute-start | bytes 3080 | tf_op jit(solution)/shard_map/ppermute | solution.py:26
  211.9 7.9 %all-to-all-start.5 = ((bf16[2,256,128]{2,0,1:T(2,128)(2,1)}), bf16[2,256,128]{2,0,1:T(2,128)(2,1)S(1)}, u32[]{:S(2)}, u32[]{:S(2)}) async-start(bf16[2,256,128]{2,0,1:T(2,128)(2,1)} %copy.61), calls=%async_computation.6 | async-start | bytes 262144 | tf_op jit(solution)/shard_map/all_to_all | solution.py:197
  219.8 7.9 %all-to-all-start.4 = ((bf16[2,256,128]{2,0,1:T(2,128)(2,1)}), bf16[2,256,128]{2,0,1:T(2,128)(2,1)S(1)}, u32[]{:S(2)}, u32[]{:S(2)}) async-start(bf16[2,256,128]{2,0,1:T(2,128)(2,1)} %copy.59), calls=%async_computation.5 | async-start | bytes 262144 | tf_op jit(solution)/shard_map/all_to_all | solution.py:190
Sparse Core Ops, SparseCore 0:
  139.0 63.7 reduce-scatter.1
